TPU v7x, 32 devices: a whole 2x2x4 slice. The times are simulated.
32 devices in a mesh: seq: 4 (over z), tp: 4 (over y, x), fsdp: 2 (over core).
Axes of the slice: x: 2, y: 2, z: 4, core: 2. Of those that a mesh axis runs over, the one named last changes fastest.
Arguments:
- decoder_in: bfloat16 [32, 128, 1024], P(('seq', 'fsdp')), may hold values from -6 to 6
- memory: bfloat16 [32, 2048, 1024], P(('seq', 'fsdp')), may hold values from -6 to 6
- buckets: int32 [128, 128], replicated, may hold values from 0 to 31
- norm_gains: bfloat16 [3, 1024], P(None, ('seq', 'fsdp')), may hold values from 0.5 to 1.5
- rel_bias: bfloat16 [32, 16], P(('seq', 'fsdp'), 'tp'), may hold values from -4 to 4
- self_q: bfloat16 [1024, 1024], P(('seq', 'fsdp'), 'tp'), may hold values from -0.1875 to 0.1875
- self_kv: bfloat16 [1024, 2, 512], P(('seq', 'fsdp'), None, 'tp'), may hold values from -0.1875 to 0.1875
- self_out: bfloat16 [1024, 1024], P('tp', ('seq', 'fsdp')), may hold values from -0.75 to 0.75
- cross_q: bfloat16 [1024, 1024], P(('seq', 'fsdp'), 'tp'), may hold values from -0.1875 to 0.1875
- cross_kv: bfloat16 [1024, 2, 512], P(('seq', 'fsdp'), None, 'tp'), may hold values from -0.1875 to 0.1875
- cross_out: bfloat16 [1024, 1024], P('tp', ('seq', 'fsdp')), may hold values from -3 to 3
- gate_up: bfloat16 [1024, 2, 2816], P(('seq', 'fsdp'), None, 'tp'), may hold values from -0.1875 to 0.1875
- down: bfloat16 [2816, 1024], P('tp', ('seq', 'fsdp')), may hold values from -0.109375 to 0.109375
- cotangent: bfloat16 [32, 128, 1024], P(('seq', 'fsdp')), may hold values from -6 to 6
Outputs:
- decoder_out: bfloat16 [32, 128, 1024], P(('seq', 'fsdp'))
- decoder_grad: float32 [32, 128, 1024], P(('seq', 'fsdp'))
- memory_grad: bfloat16 [32, 2048, 1024], P(('seq', 'fsdp'), None, 'tp')
- gains_grad: float32 [3, 1024], P(None, ('seq', 'fsdp'))
- bias_grad: float32 [32, 16], P(('seq', 'fsdp'), 'tp')
- self_q_grad: float32 [1024, 1024], P(('seq', 'fsdp'), 'tp')
- self_kv_grad: float32 [1024, 2, 512], P(('seq', 'fsdp'), None, 'tp')
- self_out_grad: float32 [1024, 1024], P('tp', ('seq', 'fsdp'))
- cross_q_grad: float32 [1024, 1024], P(('seq', 'fsdp'), 'tp')
- cross_kv_grad: float32 [1024, 2, 512], P(('seq', 'fsdp'), None, 'tp')
- cross_out_grad: float32 [1024, 1024], P('tp', ('seq', 'fsdp'))
- gate_up_grad: float32 [1024, 2, 2816], P(('seq', 'fsdp'), None, 'tp')
- down_grad: float32 [2816, 1024], P('tp', ('seq', 'fsdp'))
Inputs may be any that keep to these rules, and one draw needn't show every extreme that they name: `buckets`: the bucket of query position i and key position j, the same for every sequence and head.
All inputs are finite; a program needn't handle non-finite values.
Results may differ from a plain program's by a relative error of at most 0.04.
Values may be sent and summed in bfloat16 or wider, within the bound.
No kernel may reach another device: no remote copies, remote signals or barrier semaphores. Data moves between devices by JAX's collectives and lax.ppermute only.
A program may use at most 192 MiB of HBM per device.

v0:
```python
import jax
import jax.numpy as jnp
from jax import lax
from jax.sharding import PartitionSpec as P

DH = 64
NB = 32
EPSILON = 1e-06
MASKED = -1e30
F32 = jnp.float32
BF16 = jnp.bfloat16


def rms_norm(values, gain):
    return values * lax.rsqrt(jnp.mean(values * values, axis=-1, keepdims=True) + EPSILON) * gain


def gelu_product(gate, up):
    return jax.nn.gelu(gate, approximate=True) * up


def mm(a, b, dims):
    return lax.dot_general(a, b, (dims, ((), ())), preferred_element_type=F32)


def split_heads(query, keys, values):
    batch, rows, width = query.shape
    span = keys.shape[1]
    groups = keys.shape[2] // DH
    ratio = width // DH // groups
    return (
        query.reshape(batch, rows, groups, ratio, DH),
        keys.reshape(batch, span, groups, DH),
        values.reshape(batch, span, groups, DH),
    )


def scores_of(query_heads, key_heads, bias, causal):
    scores = jnp.einsum(
        "bigrd,bjgd->bgrij", query_heads, key_heads, preferred_element_type=F32
    ) * DH ** (-0.5)
    if bias is not None:
        scores = scores + bias
    if causal is not None:
        scores = jnp.where(causal, scores, MASKED)
    return scores


def attend_forward(query, keys, values, bias, causal):
    query_heads, key_heads, value_heads = split_heads(query, keys, values)
    scores = scores_of(query_heads, key_heads, bias, causal)
    row_max = jnp.max(scores, axis=-1, keepdims=True)
    exponent = jnp.exp(scores - row_max)
    total = jnp.sum(exponent, axis=-1, keepdims=True)
    probs = (exponent / total).astype(BF16)
    mixed = jnp.einsum("bgrij,bjgd->bigrd", probs, value_heads, preferred_element_type=F32)
    return (mixed.reshape(query.shape).astype(BF16), row_max + jnp.log(total))


def attend_backward(query, keys, values, bias, causal, log_total, grad_mixed):
    query_heads, key_heads, value_heads = split_heads(query, keys, values)
    probs = jnp.exp(scores_of(query_heads, key_heads, bias, causal) - log_total)
    grad_heads = grad_mixed.reshape(query_heads.shape)
    grad_probs = jnp.einsum(
        "bigrd,bjgd->bgrij", grad_heads, value_heads, preferred_element_type=F32
    )
    inner = jnp.sum(probs * grad_probs, axis=-1, keepdims=True)
    grad_scores = (probs * (grad_probs - inner)).astype(BF16)
    scale = DH ** (-0.5)
    grad_query = (
        jnp.einsum("bgrij,bjgd->bigrd", grad_scores, key_heads, preferred_element_type=F32) * scale
    ).astype(BF16)
    grad_keys = (
        jnp.einsum("bgrij,bigrd->bjgd", grad_scores, query_heads, preferred_element_type=F32)
        * scale
    ).astype(BF16)
    grad_values = jnp.einsum(
        "bgrij,bigrd->bjgd", probs.astype(BF16), grad_heads, preferred_element_type=F32
    ).astype(BF16)
    return (
        grad_query.reshape(query.shape),
        grad_keys.reshape(keys.shape),
        grad_values.reshape(values.shape),
        grad_scores,
    )


def per_device(
    decoder_in,
    memory,
    buckets,
    norm_gains,
    rel_bias,
    self_q,
    self_kv,
    self_out,
    cross_q,
    cross_kv,
    cross_out,
    gate_up,
    down,
    cotangent,
    tp_size,
    seq_size,
):
    batch, rows, width = decoder_in.shape
    split = tp_size // batch
    if batch * split != tp_size or rows % split:
        raise ValueError("unsupported mesh")
    chunk = rows // split
    t = lax.axis_index("tp")
    f = lax.axis_index("fsdp")
    s = lax.axis_index("seq")
    zf = ("seq", "fsdp")

    def swap_tp(x, j):
        return lax.ppermute(x, "tp", [(i, i ^ j) for i in range(tp_size)])

    def swap_core(x):
        return lax.ppermute(x, "fsdp", [(0, 1), (1, 0)])

    def exchange(pieces):
        return [pieces[0]] + [swap_tp(pieces[j], j) for j in range(1, tp_size)]

    def spread(x):
        return [x] + [swap_tp(x, j) for j in range(1, tp_size)]

    def relative(x, member, count):
        return jnp.stack([lax.dynamic_index_in_dim(x, member ^ j, 0, False) for j in range(count)])

    def piece(x, j):
        part = x[j // split]
        if split == 1:
            return part
        return lax.dynamic_slice_in_dim(part, (t % split ^ j % split) * chunk, chunk, 0)

    def pieces_of(x):
        return [piece(x, j) for j in range(tp_size)]

    def whole_rows(pieces):
        if split == 1:
            return jnp.stack(pieces)
        out = []
        for b in range(batch):
            own = jnp.stack(pieces[b * split : (b + 1) * split])
            own = relative(own, t % split, split)
            out.append(own.reshape((rows,) + own.shape[2:]))
        return jnp.stack(out)

    def placed(pieces):
        out = jnp.zeros((tp_size,) + pieces[0].shape, pieces[0].dtype)
        for j in range(tp_size):
            out = lax.dynamic_update_index_in_dim(out, pieces[j], t ^ j, 0)
        return out

    def rejoin(own, other):
        first = jnp.where(f == 0, own, other)
        second = jnp.where(f == 0, other, own)
        full = jnp.stack([first, second], axis=1)
        return full.reshape(-1, full.shape[-1])

    shard = self_q.shape[0]
    extra = jnp.zeros((4, shard), BF16)
    extra = extra.at[:3].set(norm_gains)
    tb_rows, heads = rel_bias.shape
    extra = extra.at[3, : tb_rows * heads].set(rel_bias.reshape(-1))
    extra = lax.all_gather(extra, zf, axis=0, tiled=False)
    gains = jnp.transpose(extra[:, :3], (1, 0, 2)).reshape(3, -1).astype(F32)
    table = extra[:, 3, : tb_rows * heads].reshape(NB, heads)
    pack_full = jnp.stack(
        [
            jnp.concatenate([self_out.T, cross_kv.reshape(shard, -1)], axis=1),
            jnp.concatenate([cross_q, cross_out.T], axis=1),
        ]
    )
    got_full = lax.all_gather(pack_full, "seq", axis=0, tiled=False)
    pack_self = jnp.concatenate([self_q, self_kv.reshape(shard, -1)], axis=1)
    w_self = lax.all_gather(pack_self, zf, axis=0, tiled=True)
    pack_ffn = jnp.concatenate([gate_up.reshape(shard, -1), down.T], axis=1)
    w_ffn = lax.all_gather(pack_ffn, zf, axis=0, tiled=True)
    cols = self_q.shape[1]

    def full_pair(index):
        part = got_full[:, index]
        mine = spread(part)
        theirs = [swap_core(p) for p in mine]
        joined = [rejoin(a, b) for a, b in zip(mine, theirs)]
        first = jnp.concatenate([w[:, :cols] for w in joined], axis=1)
        second = jnp.concatenate([w[:, cols:] for w in joined], axis=1)
        return (first, second)

    w_so, w_ckv = full_pair(0)
    w_cq, w_co = full_pair(1)
    positions = jnp.arange(rows, dtype=jnp.int32)
    causal = positions[:, None] >= positions[None, :]
    onehot = (buckets[:, :, None] == jnp.arange(NB, dtype=jnp.int32)[None, None, :]).astype(BF16)
    kv_half = self_kv.shape[2]
    groups = kv_half // DH
    bias = jnp.einsum("ijn,nh->hij", onehot, table, preferred_element_type=F32).reshape(
        groups, heads // groups, rows, rows
    )
    tokens = relative(decoder_in, t // split, batch)
    start = tokens.astype(F32)
    normed_self = rms_norm(start, gains[0]).astype(BF16)
    proj = mm(normed_self, w_self, ((2,), (0,))).astype(BF16)
    query_self = proj[..., :cols]
    keys_self = proj[..., cols : cols + kv_half]
    values_self = proj[..., cols + kv_half :]
    mixed_self, log_self = attend_forward(query_self, keys_self, values_self, bias, causal)
    o1 = jnp.concatenate(exchange(pieces_of(mixed_self)), axis=-1)
    x0 = piece(start, 0)
    x1 = x0 + mm(o1, w_so, ((1,), (1,)))
    n2 = rms_norm(x1, gains[1]).astype(BF16)
    q2 = mm(n2, w_cq, ((1,), (0,))).astype(BF16)
    own_memory = lax.dynamic_index_in_dim(memory, t // split, 0, False)
    kv2 = mm(own_memory, w_ckv, ((1,), (0,))).astype(BF16)
    span = kv2.shape[0]
    kv2 = kv2.reshape(span, tp_size, 2, kv_half)
    k2 = kv2[:, :, 0].reshape(1, span, -1)
    v2 = kv2[:, :, 1].reshape(1, span, -1)
    o2, log_cross = attend_forward(q2[None], k2, v2, None, None)
    x2 = x1 + mm(o2[0], w_co, ((1,), (1,)))
    n3 = rms_norm(x2, gains[2]).astype(BF16)
    n3_all = jnp.stack(spread(n3)).reshape(-1, width)
    ff2 = gate_up.shape[2] * 2
    hid = gate_up.shape[2]
    w_gu = w_ffn[:, :ff2]
    w_dn = w_ffn[:, ff2:]
    joined = mm(n3_all, w_gu, ((1,), (0,)))
    gate = joined[:, :hid]
    up = joined[:, hid:]
    hidden = gelu_product(gate, up).astype(BF16)
    out_part = mm(hidden, w_dn, ((1,), (1,))).astype(BF16).reshape(tp_size, chunk, width)
    cot = relative(cotangent.reshape(tp_size, chunk, width), t, tp_size)
    y3 = cot.reshape(-1, width)
    grad_hidden = mm(y3, w_dn, ((1,), (0,)))
    _, pull = jax.vjp(gelu_product, gate, up)
    grad_gate, grad_up = pull(grad_hidden)
    grad_joined = jnp.concatenate([grad_gate, grad_up], axis=-1).astype(BF16)
    dn3_part = mm(grad_joined, w_gu, ((1,), (1,))).astype(BF16).reshape(tp_size, chunk, width)

    def total(pieces):
        acc = pieces[0].astype(F32)
        for p in pieces[1:]:
            acc = acc + p.astype(F32)
        return acc

    dn3 = total(exchange([dn3_part[j] for j in range(tp_size)]))
    out = x2 + total(exchange([out_part[j] for j in range(tp_size)]))
    decoder_out = placed(spread(out.astype(BF16))).reshape(decoder_in.shape)
    gu_grad = mm(n3_all, grad_joined, ((0,), (0,))).astype(BF16)
    dn_grad = mm(y3, hidden, ((0,), (0,))).astype(BF16)
    ffn_grad = lax.psum_scatter(
        jnp.concatenate([gu_grad, dn_grad], axis=1), zf, scatter_dimension=0, tiled=True
    )
    e3 = cot[0].astype(F32)
    _, pull = jax.vjp(rms_norm, x2, gains[2])
    dv, dg2 = pull(dn3)
    e2 = e3 + dv
    y2 = e2.astype(BF16)
    do2 = mm(y2, w_co, ((1,), (0,))).astype(BF16)
    dq2, dk2, dv2, _ = attend_backward(q2[None], k2, v2, None, None, log_cross, do2[None])
    dq2 = dq2[0]
    dkv2 = jnp.stack(
        [dk2[0].reshape(span, tp_size, kv_half), dv2[0].reshape(span, tp_size, kv_half)], axis=2
    ).reshape(span, -1)
    dn2 = mm(dq2, w_cq, ((1,), (1,)))
    _, pull = jax.vjp(rms_norm, x1, gains[1])
    dv, dg1 = pull(dn2)
    e1 = e2 + dv
    y1 = e1.astype(BF16)
    do1_full = mm(y1, w_so, ((1,), (0,))).astype(BF16)
    do1 = whole_rows(exchange([do1_full[:, j * cols : (j + 1) * cols] for j in range(tp_size)]))
    quarter = width // tp_size
    w_rows = w_ckv.reshape(tp_size, quarter, -1)
    mem_pieces = []
    for j in range(tp_size):
        w_j = lax.dynamic_index_in_dim(w_rows, t ^ j, 0, False)
        mem_pieces.append(mm(dkv2, w_j, ((1,), (1,))).astype(BF16))
    mem_got = exchange(mem_pieces)
    memory_grad = jnp.zeros((batch,) + mem_got[0].shape, BF16)
    for b in range(batch):
        own = mem_got[b * split]
        if split > 1:
            own = total(mem_got[b * split : (b + 1) * split]).astype(BF16)
        memory_grad = lax.dynamic_update_index_in_dim(memory_grad, own, t // split ^ b, 0)

    def core_sum(grad):
        g = grad.reshape(seq_size, 2, shard, -1)
        mine = lax.dynamic_index_in_dim(g, f, 1, False)
        theirs = lax.dynamic_index_in_dim(g, 1 - f, 1, False)
        return (mine.astype(F32) + swap_core(theirs).astype(F32)).astype(BF16)

    def tp_sum(parts):
        pieces = [
            jnp.concatenate([p[..., j * cols : (j + 1) * cols] for p in parts], axis=-1)
            for j in range(tp_size)
        ]
        return total(exchange(pieces)).astype(BF16)

    g_co = core_sum(mm(y2, o2[0], ((0,), (0,))).astype(BF16))
    g_cq = core_sum(mm(n2, dq2, ((0,), (0,))).astype(BF16))
    g_ckv = core_sum(mm(own_memory, dkv2, ((0,), (0,))).astype(BF16))
    g_so = core_sum(mm(y1, o1, ((0,), (0,))).astype(BF16))
    full_grad = tp_sum([g_co, g_cq, g_ckv, g_so])
    full_grad = lax.psum_scatter(full_grad, "seq", scatter_dimension=0, tiled=False)
    dq1, dk1, dv1, ds1 = attend_backward(
        query_self, keys_self, values_self, bias, causal, log_self, do1
    )
    table_grad = jnp.einsum(
        "ijn,bhij->nh", onehot, ds1.reshape(batch, -1, rows, rows), preferred_element_type=F32
    )
    dproj = jnp.concatenate([dq1, dk1, dv1], axis=-1)
    dn1_part = mm(dproj, w_self, ((2,), (1,))).astype(BF16)
    self_grad = lax.psum_scatter(
        mm(normed_self.reshape(-1, width), dproj.reshape(-1, dproj.shape[-1]), ((0,), (0,))).astype(
            BF16
        ),
        zf,
        scatter_dimension=0,
        tiled=True,
    )
    dn1 = total(exchange(pieces_of(dn1_part)))
    _, pull = jax.vjp(rms_norm, x0, gains[0])
    dv, dg0 = pull(dn1)
    decoder_grad = placed(spread((e1 + dv).astype(BF16))).reshape(decoder_in.shape).astype(F32)
    small = jnp.stack([dg0, dg1, dg2, jnp.pad(table_grad.reshape(-1), (0, width - NB * heads))])
    small = lax.all_gather(small, ("seq", "fsdp", "tp"), axis=0, tiled=False)
    place = s * 2 + f
    gains_grad = lax.dynamic_slice_in_dim(jnp.sum(small[:, :3], axis=0), place * shard, shard, 1)
    tables = small[:, 3, : NB * heads].reshape(-1, tp_size, NB * heads)
    tables = jnp.sum(lax.dynamic_index_in_dim(tables, t, 1, False), axis=0).reshape(NB, heads)
    bias_grad = lax.dynamic_slice_in_dim(tables, place * tb_rows, tb_rows, 0)
    full_grad = full_grad.astype(F32)
    self_grad = self_grad.astype(F32)
    ffn_grad = ffn_grad.astype(F32)
    return (
        decoder_out,
        decoder_grad,
        memory_grad,
        gains_grad,
        bias_grad,
        self_grad[:, :cols],
        self_grad[:, cols:].reshape(self_kv.shape),
        full_grad[:, 3 * cols :].T,
        full_grad[:, cols : 2 * cols],
        full_grad[:, 2 * cols : 3 * cols].reshape(cross_kv.shape),
        full_grad[:, :cols].T,
        ffn_grad[:, :ff2].reshape(gate_up.shape),
        ffn_grad[:, ff2:].T,
    )


def solution(mesh):
    tp_size = mesh.shape["tp"]
    seq_size = mesh.shape["seq"]

    def body(*args):
        return per_device(*args, tp_size=tp_size, seq_size=seq_size)

    both = ("seq", "fsdp")
    token = P(both, None, None)
    weight = P(both, "tp")
    paired = P(both, None, "tp")
    turned = P("tp", both)
    return jax.shard_map(
        body,
        mesh=mesh,
        in_specs=(
            token,
            token,
            P(),
            P(None, both),
            weight,
            weight,
            paired,
            turned,
            weight,
            paired,
            turned,
            paired,
            turned,
            token,
        ),
        out_specs=(
            token,
            token,
            P(both, None, "tp"),
            P(None, both),
            weight,
            weight,
            paired,
            turned,
            weight,
            paired,
            turned,
            paired,
            turned,
        ),
        check_vma=False,
    )
```

profile of v0, /device:TPU:0, one launch (start us, length us, event | category | flops | bytes accessed | tf_op | source)
XLA Modules:
  0.0 551.6 jit_solution(9025525953042338345)
XLA Ops:
  15.4 13.5 %all_gather.28 = bf16[8,4,128]{2,1,0:T(4,128)(2,1)S(1)} all-gather(bf16[1,4,128]{2,1,0:T(4,128)(2,1)S(1)} %scatter.9), channel_id=1, replica_groups=mesh['seq'=4,'tp'=4,'fsdp'=2] {'seq','fsdp'}, dimensions={0}, use_global_device_ids=true | all-gather | bytes 9216 | tf_op jit(solution)/shard_map/all_gather | solution.py:167
  34.0 8.6 %all-gather.11.cloned.1.call-done = bf16[8,128,512]{2,1,0:T(8,128)(2,1)} async-done(((bf16[2,128,512]{2,1,0:T(8,128)(2,1)}), bf16[8,128,512]{2,1,0:T(8,128)(2,1)}) %all-gather.11.cloned.1.call-update) | async-done | bytes 1048592 | tf_op jit(solution)/shard_map/all_gather | solution.py:176
  48.9 17.2 %all-gather.7.cloned.1.call-done = bf16[1024,512]{1,0:T(8,128)(2,1)} async-done(((bf16[128,512]{1,0:T(8,128)(2,1)}), bf16[1024,512]{1,0:T(8,128)(2,1)}) %all-gather.7.cloned.1.call-update) | async-done | bytes 1048592 | tf_op jit(solution)/shard_map/all_gather | solution.py:178
  93.7 8.1 %collective-permute-done.13 = bf16[4,128,512]{2,1,0:T(8,128)(2,1)S(1)} collective-permute-done((bf16[4,128,512]{2,1,0:T(8,128)(2,1)}, bf16[4,128,512]{2,1,0:T(8,128)(2,1)S(1)}, u32[]{:S(2)}, u32[]{:S(2)}) %collective-permute-start.13) | collective-permute-done | bytes 524320 | tf_op jit(solution)/shard_map/ppermute | solution.py:117
  112.4 7.5 %fusion.21 = bf16[2048,1024]{0,1:T(8,128)(2,1)S(1)} fusion(bf16[4,2048,1024]{2,1,0:T(8,128)(2,1)} %param.19, s32[]{:T(128)S(6)} %select_n.140, bf16[1024,256]{1,0:T(8,128)(2,1)S(1)} %get-tuple-element.184, bf16[1024,256]{1,0:T(8,128)(2,1)S(1)} %copy-done.39, bf16[1024,256]{1,0:T(8,128)(2,1)S(1)} %copy-done.40, bf16[1024,256]{1,0:T(8,128)(2,1)S(1)} %get-tuple-element.178), kind=kOutput, calls=%fused_computation.31 | convolution fusion | flops 4305453056 | bytes 10485764 | tf_op jit(solution)/shard_map/dot_general | solution.py:23
  120.3 8.2 %bitcast_reduce_fusion = (f32[8,2,128]{2,1,0:T(2,128)S(1)}, f32[8,2048,128,2]{2,1,3,0:T(8,128)}) fusion(bf16[2048,8,64,1]{0,2,3,1:T(8,128)(2,1)S(1)} %bitcast.415, bf16[128,8,2,64]{0,3,2,1:T(8,128)(2,1)S(1)} %bitcast.424), kind=kOutput, calls=%fused_computation.7 | convolution fusion | flops 545257472 | bytes 19144704 | tf_op jit(solution)/shard_map/bigrd,bjgd->bgrij/dot_general | solution.py:39
  128.5 8.6 %fusion.5 = f32[8,2,128]{2,1,0:T(2,128)S(1)} fusion(f32[8,2048,128,2]{2,1,3,0:T(8,128)} %get-tuple-element.220, f32[8,2,128]{2,1,0:T(2,128)S(1)} %get-tuple-element.219), kind=kLoop, calls=%fused_computation.11 | loop fusion | flops 12580864 | bytes 16793600 | tf_op jit(solution)/shard_map/reduce_sum | solution.py:54
  137.1 7.7 %fusion.63 = bf16[8,64,2,128]{3,1,2,0:T(8,128)(2,1)S(1)} fusion(bf16[2048,8,64,1]{0,2,3,1:T(8,128)(2,1)S(1)} %bitcast.421, f32[8,2,128]{2,1,0:T(2,128)S(1)} %fusion.5, f32[8,2,128]{2,1,0:T(2,128)S(1)} %get-tuple-element.219, f32[8,2048,128,2]{2,1,3,0:T(8,128)} %get-tuple-element.220), kind=kOutput, calls=%fused_computation.104 | convolution fusion | flops 553779200 | bytes 19152896 | tf_op jit(solution)/shard_map/bgrij,bjgd->bigrd/dot_general | solution.py:56
  151.5 5.4 collective-permute-done.19
  156.9 4.8 collective-permute-done.18
  163.8 4.1 fusion.30
  176.4 6.6 %collective-permute-done.28 = bf16[128,1024]{1,0:T(8,128)(2,1)S(1)} collective-permute-done((bf16[128,1024]{1,0:T(8,128)(2,1)S(1)}, bf16[128,1024]{1,0:T(8,128)(2,1)S(1)}, u32[]{:S(2)}, u32[]{:S(2)}) %collective-permute-start.28) | collective-permute-done | bytes 262176 | tf_op jit(solution)/shard_map/ppermute | solution.py:117
  182.9 4.6 collective-permute-done.27
  191.6 11.9 %fusion = (f32[8,2,128]{2,1,0:T(2,128)S(1)}, f32[8,2048,128,2]{2,1,3,0:T(8,128)}) fusion(f32[8,2048,128,2]{2,1,3,0:T(8,128)} %get-tuple-element.220, f32[8,2,128]{2,1,0:T(2,128)S(1)} %bitcast.490, bf16[2048,8,64,1]{0,2,3,1:T(8,128)(2,1)} %bitcast.422, bf16[128,8,2,64]{0,3,2,1:T(8,128)(2,1)} %bitcast.442), kind=kOutput, calls=%fused_computation.2 | convolution fusion | flops 553646080 | bytes 35930112 | tf_op jit(solution)/shard_map/bigrd,bjgd->bgrij/dot_general | solution.py:64
  203.5 10.1 %bitcast_convert_fusion = bf16[8,64,2048]{2,1,0:T(8,128)(2,1)} fusion(bf16[128,8,2,64]{0,3,2,1:T(8,128)(2,1)S(1)} %bitcast.443, f32[8,2048,128,2]{2,1,3,0:T(8,128)} %get-tuple-element.220, f32[8,2,128]{2,1,0:T(2,128)S(1)} %bitcast.491), kind=kOutput, calls=%fused_computation.23 | convolution fusion | flops 550502400 | bytes 19144704 | tf_op jit(solution)/shard_map/bgrij,bigrd->bjgd/dot_general | solution.py:77
  213.6 12.0 %fusion.10 = bf16[8,2,128,2048]{2,3,1,0:T(8,128)(2,1)S(1)} fusion(f32[8,2048,128,2]{2,1,3,0:T(8,128)} %get-tuple-element.224, f32[8,2048,128,2]{2,1,3,0:T(8,128)} %get-tuple-element.220, f32[8,2,128]{2,1,0:T(2,128)S(1)} %get-tuple-element.223, f32[8,2,128]{2,1,0:T(2,128)S(1)} %bitcast.492), kind=kLoop, calls=%fused_computation.15 | loop fusion | flops 20971520 | bytes 41959424 | tf_op jit(solution)/shard_map/reshape.150
  248.1 8.6 %fusion.42 = bf16[1024,1024]{1,0:T(8,128)(2,1)S(1)} fusion(bf16[2048,1024]{0,1:T(8,128)(2,1)S(1)} %bitcast.428, bf16[4,2048,1024]{2,1,0:T(8,128)(2,1)} %param.19, s32[]{:T(128)S(6)} %select_n.140), kind=kOutput, calls=%fused_computation.66 | convolution fusion | flops 4296015872 | bytes 10485764 | tf_op jit(solution)/shard_map/dot_general | solution.py:23
  297.9 23.2 %collective-permute-done.47 = bf16[4,128,1024]{1,2,0:T(8,128)(2,1)S(1)} collective-permute-done((bf16[4,128,1024]{1,2,0:T(8,128)(2,1)S(1)}, bf16[4,128,1024]{1,2,0:T(8,128)(2,1)S(1)}, u32[]{:S(2)}, u32[]{:S(2)}) %collective-permute-start.47) | collective-permute-done | bytes 1048608 | tf_op jit(solution)/shard_map/ppermute | solution.py:117
  321.1 21.5 %collective-permute-done.46 = bf16[4,128,1024]{1,2,0:T(8,128)(2,1)S(1)} collective-permute-done((bf16[4,128,1024]{1,2,0:T(8,128)(2,1)S(1)}, bf16[4,128,1024]{1,2,0:T(8,128)(2,1)S(1)}, u32[]{:S(2)}, u32[]{:S(2)}) %collective-permute-start.46) | collective-permute-done | bytes 1048608 | tf_op jit(solution)/shard_map/ppermute | solution.py:117
  367.1 4.9 collective-permute-done.22
  371.9 4.7 collective-permute-done.21
  410.6 11.7 %collective-permute-done.34 = bf16[128,1024]{1,0:T(8,128)(2,1)S(1)} collective-permute-done((bf16[128,1024]{1,0:T(8,128)(2,1)}, bf16[128,1024]{1,0:T(8,128)(2,1)S(1)}, u32[]{:S(2)}, u32[]{:S(2)}) %collective-permute-start.34) | collective-permute-done | bytes 262176 | tf_op jit(solution)/shard_map/ppermute | solution.py:117
  433.5 83.1 %all-gather.2 = f32[32,4,1024]{2,1,0:T(4,128)S(1)} all-gather(f32[1,4,1024]{2,1,0:T(4,128)S(1)} %maximum_bitcast_fusion.2), channel_id=3, replica_groups=mesh['seq'=4,'tp'=4,'fsdp'=2] {'seq','fsdp','tp'}, dimensions={0}, use_global_device_ids=true | all-gather | bytes 540672 | tf_op jit(solution)/shard_map/all_gather | solution.py:328
  519.4 5.8 %collective-permute-done.37 = bf16[128,1024]{1,0:T(8,128)(2,1)S(1)} collective-permute-done((bf16[128,1024]{1,0:T(8,128)(2,1)S(1)}, bf16[128,1024]{1,0:T(8,128)(2,1)S(1)}, u32[]{:S(2)}, u32[]{:S(2)}) %collective-permute-start.37) | collective-permute-done | bytes 262176 | tf_op jit(solution)/shard_map/ppermute | solution.py:117
  (502 shorter events, 232.8 us)
Async XLA Ops:
  7.2 35.4 %all-gather.11.cloned.1.call-start = ((), (), s32[]{:S(2)}) async-start(), calls=%async_computation.8 | async-start | bytes 1310720 | tf_op jit(solution)/shard_map/all_gather | solution.py:176
  11.7 54.3 %all-gather.7.cloned.1.call-start = ((), (), s32[]{:S(2)}) async-start(), calls=%async_computation.3 | async-start | bytes 1179648 | tf_op jit(solution)/shard_map/all_gather | solution.py:178
  14.2 149.6 %all-gather.9.cloned.1.call-start = ((), (), s32[]{:S(2)}) async-start(), calls=%async_computation.4 | async-start | bytes 4866048 | tf_op jit(solution)/shard_map/all_gather | solution.py:180
  15.1 520.5 %reduce-scatter.4.cloned.1.call-start = ((), (), s32[]{:S(2)}) async-start(), calls=%async_computation.5 | async-start | bytes 1179648 | tf_op jit(solution)/shard_map/reduce_scatter | solution.py:315
  44.9 34.6 %collective-permute-start.8 = (bf16[4,128,512]{2,1,0:T(8,128)(2,1)}, bf16[4,128,512]{2,1,0:T(8,128)(2,1)}, u32[]{:S(2)}, u32[]{:S(2)}) collective-permute-start(bf16[4,128,512]{2,1,0:T(8,128)(2,1)} %get-tuple-element.177), channel_id=1, source_target_pairs={{0,6},{2,4},{4,2},{6,0},{1,7},{3,5},{5,3},{7,1},{8,14},{10,12},{12... | collective-permute-start | bytes 1572872 | tf_op jit(solution)/shard_map/ppermute | solution.py:117
  47.3 32.3 %collective-permute-start.6 = (bf16[4,128,512]{2,1,0:T(8,128)(2,1)}, bf16[4,128,512]{2,1,0:T(8,128)(2,1)}, u32[]{:S(2)}, u32[]{:S(2)}) collective-permute-start(bf16[4,128,512]{2,1,0:T(8,128)(2,1)} %get-tuple-element.177), channel_id=1, source_target_pairs={{0,4},{2,6},{4,0},{6,2},{1,5},{3,7},{5,1},{7,3},{8,12},{10,14},{12... | collective-permute-start | bytes 1572872 | tf_op jit(solution)/shard_map/ppermute | solution.py:117
  47.8 33.3 %collective-permute-start.4 = (bf16[4,128,512]{2,1,0:T(8,128)(2,1)}, bf16[4,128,512]{2,1,0:T(8,128)(2,1)}, u32[]{:S(2)}, u32[]{:S(2)}) collective-permute-start(bf16[4,128,512]{2,1,0:T(8,128)(2,1)} %get-tuple-element.177), channel_id=1, source_target_pairs={{0,2},{2,0},{4,6},{6,4},{1,3},{3,1},{5,7},{7,5},{8,10},{10,8},{12,... | collective-permute-start | bytes 1572872 | tf_op jit(solution)/shard_map/ppermute | solution.py:117
  48.4 28.7 %collective-permute-start.3 = (bf16[4,128,512]{2,1,0:T(8,128)(2,1)}, bf16[4,128,512]{2,1,0:T(8,128)(2,1)}, u32[]{:S(2)}, u32[]{:S(2)}) collective-permute-start(bf16[4,128,512]{2,1,0:T(8,128)(2,1)} %get-tuple-element.177), channel_id=1, source_target_pairs={{0,1},{1,0},{2,3},{3,2},{4,5},{5,4},{6,7},{7,6},{8,9},{9,8},{10,11... | collective-permute-start | bytes 1572872 | tf_op jit(solution)/shard_map/ppermute | solution.py:120
  48.4 26.2 %collective-permute-start.10 = (bf16[4,128,512]{2,1,0:T(8,128)(2,1)}, bf16[4,128,512]{2,1,0:T(8,128)(2,1)}, u32[]{:S(2)}, u32[]{:S(2)}) collective-permute-start(bf16[4,128,512]{2,1,0:T(8,128)(2,1)} %get-tuple-element.176), channel_id=1, source_target_pairs={{0,1},{1,0},{2,3},{3,2},{4,5},{5,4},{6,7},{7,6},{8,9},{9,8},{10,11... | collective-permute-start | bytes 1572872 | tf_op jit(solution)/shard_map/ppermute | solution.py:120
  238.0 37.4 %collective-permute-start.31 = (bf16[128,256]{1,0:T(8,128)(2,1)}, bf16[128,256]{1,0:T(8,128)(2,1)}, u32[]{:S(2)}, u32[]{:S(2)}) collective-permute-start(bf16[128,256]{1,0:T(8,128)(2,1)} %get-tuple-element.203), channel_id=1, source_target_pairs={{0,6},{2,4},{4,2},{6,0},{1,7},{3,5},{5,3},{7,1},{8,14},{10,12},{12... | collective-permute-start | bytes 196616 | tf_op jit(solution)/shard_map/ppermute | solution.py:117
  239.5 36.9 %collective-permute-start.30 = (bf16[128,256]{1,0:T(8,128)(2,1)}, bf16[128,256]{1,0:T(8,128)(2,1)}, u32[]{:S(2)}, u32[]{:S(2)}) collective-permute-start(bf16[128,256]{1,0:T(8,128)(2,1)} %get-tuple-element.204), channel_id=1, source_target_pairs={{0,4},{2,6},{4,0},{6,2},{1,5},{3,7},{5,1},{7,3},{8,12},{10,14},{12... | collective-permute-start | bytes 196616 | tf_op jit(solution)/shard_map/ppermute | solution.py:117
  240.1 37.8 %collective-permute-start.29 = (bf16[128,256]{1,0:T(8,128)(2,1)}, bf16[128,256]{1,0:T(8,128)(2,1)S(1)}, u32[]{:S(2)}, u32[]{:S(2)}) collective-permute-start(bf16[128,256]{1,0:T(8,128)(2,1)} %get-tuple-element.205), channel_id=1, source_target_pairs={{0,2},{2,0},{4,6},{6,4},{1,3},{3,1},{5,7},{7,5},{8,10},{10,8},{12,... | collective-permute-start | bytes 196616 | tf_op jit(solution)/shard_map/ppermute | solution.py:117
  246.1 41.3 %collective-permute-start.44 = (bf16[4,128,1024]{1,2,0:T(8,128)(2,1)}, bf16[4,128,1024]{1,2,0:T(8,128)(2,1)}, u32[]{:S(2)}, u32[]{:S(2)}) collective-permute-start(bf16[4,128,1024]{1,2,0:T(8,128)(2,1)} %bitcast.458), channel_id=1, source_target_pairs={{0,1},{1,0},{2,3},{3,2},{4,5},{5,4},{6,7},{7,6},{8,9},{9,8},{10,11... | collective-permute-start | bytes 3145736 | tf_op jit(solution)/shard_map/ppermute | solution.py:120
  260.8 28.3 %collective-permute-start.43 = (bf16[4,128,1024]{1,2,0:T(8,128)(2,1)}, bf16[4,128,1024]{1,2,0:T(8,128)(2,1)}, u32[]{:S(2)}, u32[]{:S(2)}) collective-permute-start(bf16[4,128,1024]{1,2,0:T(8,128)(2,1)} %bitcast.459), channel_id=1, source_target_pairs={{0,1},{1,0},{2,3},{3,2},{4,5},{5,4},{6,7},{7,6},{8,9},{9,8},{10,11... | collective-permute-start | bytes 3145736 | tf_op jit(solution)/shard_map/ppermute | solution.py:120
  287.3 250.5 %reduce-scatter.6.cloned.1.call-start = ((), (), s32[]{:S(2)}) async-start(), calls=%async_computation.6 | async-start | bytes 1310720 | tf_op jit(solution)/shard_map/reduce_scatter | solution.py:306
  294.1 27.0 %collective-permute-start.47 = (bf16[4,128,1024]{1,2,0:T(8,128)(2,1)S(1)}, bf16[4,128,1024]{1,2,0:T(8,128)(2,1)S(1)}, u32[]{:S(2)}, u32[]{:S(2)}) collective-permute-start(bf16[4,128,1024]{1,2,0:T(8,128)(2,1)S(1)} %pad_maximum_fusion.19), channel_id=1, source_target_pairs={{0,6},{2,4},{4,2},{6,0},{1,7},{3,5},{5,3},{7,1},{8,14},{10,12},{12... | collective-permute-start | bytes 3145736 | tf_op jit(solution)/shard_map/ppermute | solution.py:117
  295.7 46.9 %collective-permute-start.46 = (bf16[4,128,1024]{1,2,0:T(8,128)(2,1)S(1)}, bf16[4,128,1024]{1,2,0:T(8,128)(2,1)S(1)}, u32[]{:S(2)}, u32[]{:S(2)}) collective-permute-start(bf16[4,128,1024]{1,2,0:T(8,128)(2,1)S(1)} %pad_maximum_fusion.18), channel_id=1, source_target_pairs={{0,4},{2,6},{4,0},{6,2},{1,5},{3,7},{5,1},{7,3},{8,12},{10,14},{12... | collective-permute-start | bytes 3145736 | tf_op jit(solution)/shard_map/ppermute | solution.py:117
  296.4 46.2 %collective-permute-start.45 = (bf16[4,128,1024]{1,2,0:T(8,128)(2,1)S(1)}, bf16[4,128,1024]{1,2,0:T(8,128)(2,1)S(1)}, u32[]{:S(2)}, u32[]{:S(2)}) collective-permute-start(bf16[4,128,1024]{1,2,0:T(8,128)(2,1)S(1)} %pad_maximum_fusion.17), channel_id=1, source_target_pairs={{0,2},{2,0},{4,6},{6,4},{1,3},{3,1},{5,7},{7,5},{8,10},{10,8},{12,... | collective-permute-start | bytes 3145736 | tf_op jit(solution)/shard_map/ppermute | solution.py:117
  344.2 196.9 %reduce-scatter.8.cloned.1.call-start = ((), (), s32[]{:S(2)}) async-start(), calls=%async_computation.7 | async-start | bytes 5013504 | tf_op jit(solution)/shard_map/reduce_scatter | solution.py:253
  385.1 143.7 %collective-permute-start.38 = (bf16[2048,256]{1,0:T(8,128)(2,1)}, bf16[2048,256]{1,0:T(8,128)(2,1)}, u32[]{:S(2)}, u32[]{:S(2)}) collective-permute-start(bf16[2048,256]{1,0:T(8,128)(2,1)} %convolution_convert_fusion.3), channel_id=1, source_target_pairs={{0,2},{2,0},{4,6},{6,4},{1,3},{3,1},{5,7},{7,5},{8,10},{10,8},{12,... | collective-permute-start | bytes 3145736 | tf_op jit(solution)/shard_map/ppermute | solution.py:117
  407.5 123.5 %collective-permute-start.39 = (bf16[2048,256]{1,0:T(8,128)(2,1)}, bf16[2048,256]{1,0:T(8,128)(2,1)}, u32[]{:S(2)}, u32[]{:S(2)}) collective-permute-start(bf16[2048,256]{1,0:T(8,128)(2,1)} %convolution_convert_fusion.2), channel_id=1, source_target_pairs={{0,4},{2,6},{4,0},{6,2},{1,5},{3,7},{5,1},{7,3},{8,12},{10,14},{12... | collective-permute-start | bytes 3145736 | tf_op jit(solution)/shard_map/ppermute | solution.py:117
  422.3 111.0 %collective-permute-start.40 = (bf16[2048,256]{1,0:T(8,128)(2,1)}, bf16[2048,256]{1,0:T(8,128)(2,1)}, u32[]{:S(2)}, u32[]{:S(2)}) collective-permute-start(bf16[2048,256]{1,0:T(8,128)(2,1)} %convolution_convert_fusion.1), channel_id=1, source_target_pairs={{0,6},{2,4},{4,2},{6,0},{1,7},{3,5},{5,3},{7,1},{8,14},{10,12},{12... | collective-permute-start | bytes 3145736 | tf_op jit(solution)/shard_map/ppermute | solution.py:117
  431.4 86.6 %collective-permute-start.35 = (bf16[128,1024]{1,0:T(8,128)(2,1)S(1)}, bf16[128,1024]{1,0:T(8,128)(2,1)S(1)}, u32[]{:S(2)}, u32[]{:S(2)}) collective-permute-start(bf16[128,1024]{1,0:T(8,128)(2,1)S(1)} %get-tuple-element.111), channel_id=1, source_target_pairs={{0,2},{2,0},{4,6},{6,4},{1,3},{3,1},{5,7},{7,5},{8,10},{10,8},{12,... | collective-permute-start | bytes 786440 | tf_op jit(solution)/shard_map/ppermute | solution.py:117
  432.1 86.6 %collective-permute-start.36 = (bf16[128,1024]{1,0:T(8,128)(2,1)S(1)}, bf16[128,1024]{1,0:T(8,128)(2,1)S(1)}, u32[]{:S(2)}, u32[]{:S(2)}) collective-permute-start(bf16[128,1024]{1,0:T(8,128)(2,1)S(1)} %get-tuple-element.111), channel_id=1, source_target_pairs={{0,4},{2,6},{4,0},{6,2},{1,5},{3,7},{5,1},{7,3},{8,12},{10,14},{12... | collective-permute-start | bytes 786440 | tf_op jit(solution)/shard_map/ppermute | solution.py:117
  (136 other events, 1481.5 us)
Sparse Core Ops, SparseCore 0:
  11.9 30.7 all-gather.10
  44.8 21.2 all-gather.6
  68.2 48.8 all-gather.8
  287.4 31.6 reduce-scatter.3
  344.3 26.2 reduce-scatter.5
  372.8 50.8 reduce-scatter.7
where the time goes:
time: 560 us; the launch traced here: 552 us
  waiting for transfers between devices  136 us (24%)
  matrix products  109 us (19%)
  blocking collectives  96.6 us (17%)
  local copies, waits for them, and re-layouts  85.9 us (15%)
  other arithmetic  62.1 us (11%)
  starting transfers between devices  45.6 us (8%)
  between operations  16.4 us (3%)
    ppermute x36, waiting for transfers between devices, swap_tp(): return lax.ppermute(x, 'tp', [(i, i ^ j) for i in range(tp_size)])  110 us
    all_gather x1, blocking collectives, per_device(): small = lax.all_gather(small, ('seq', 'fsdp', 'tp'), axis=0, tiled=False)  83.1 us
    dot_general x24, matrix products, mm(): return lax.dot_general(a, b, (dims, ((), ())), preferred_element_type=F32)  60.5 us
    ppermute x36, starting transfers between devices, swap_tp(): return lax.ppermute(x, 'tp', [(i, i ^ j) for i in range(tp_size)])  42.6 us
    unnamed x223, local copies, waits for them, and re-layouts  20.3 us
    all_gather x1, waiting for transfers between devices, per_device(): w_self = lax.all_gather(pack_self, zf, axis=0, tiled=True)  17.2 us
    all_gather x1, blocking collectives, per_device(): extra = lax.all_gather(extra, zf, axis=0, tiled=False)  13.5 us
    dot_general x2, matrix products, attend_backward(): jnp.einsum('bigrd,bjgd->bgrij', grad_heads, value_heads, preferred_elemen...  13.2 us
  transfers between devices with their start and end apart: 54, of which 15 were waited for; matrix products, arithmetic and copies ran while one was open for 33% of the time, Pallas kernels for 0%

commit v1 on v0

--- a/solution.py
+++ b/solution.py
@@ -175,9 +175,12 @@
     )
     got_full = lax.all_gather(pack_full, "seq", axis=0, tiled=False)
     pack_self = jnp.concatenate([self_q, self_kv.reshape(shard, -1)], axis=1)
-    w_self = lax.all_gather(pack_self, zf, axis=0, tiled=True)
     pack_ffn = jnp.concatenate([gate_up.reshape(shard, -1), down.T], axis=1)
-    w_ffn = lax.all_gather(pack_ffn, zf, axis=0, tiled=True)
+    w_self, w_ffn = jnp.split(
+        lax.all_gather(jnp.concatenate([pack_self, pack_ffn], axis=1), zf, axis=0, tiled=True),
+        [pack_self.shape[1]],
+        axis=1,
+    )
     cols = self_q.shape[1]
 
     def full_pair(index):

time: 560 us -> 570 us (1.018)
  other arithmetic: 62.1 us -> 50.4 us
  matrix products: 109 us -> 119 us
  waiting for transfers between devices: 136 us -> 146 us
    ppermute x36, waiting for transfers between devices: 110 us -> 136 us  [swap_tp(): return lax.ppermute(x, 'tp', [(i, i ^ j) for i in range(tp_size)])]
    all_gather x2 -> x1, waiting for transfers between devices: 17.2 us -> 0.01 us  [per_device(): lax.all_gather(jnp.concatenate([pack_self, pack_ffn], axis=1), zf, axis=0...]
    unnamed x223 -> x282, local copies, waits for them, and re-layouts: 20.3 us -> 23.2 us
  transfers between devices with their start and end apart: 54 -> 53, of which waited for: 15 -> 24; matrix products, arithmetic and copies ran while one was open for 33% -> 25% of each run, Pallas kernels for 0% -> 0%
where the time goes in v1:
time: 570 us; the launch traced here: 563 us
  waiting for transfers between devices  146 us (26%)
  matrix products  119 us (21%)
  blocking collectives  95.7 us (17%)
  local copies, waits for them, and re-layouts  91.2 us (16%)
  other arithmetic  50.4 us (9%)
  starting transfers between devices  44.3 us (8%)
  between operations  16.3 us (3%)
    ppermute x36, waiting for transfers between devices, swap_tp(): return lax.ppermute(x, 'tp', [(i, i ^ j) for i in range(tp_size)])  136 us
    all_gather x1, blocking collectives, per_device(): small = lax.all_gather(small, ('seq', 'fsdp', 'tp'), axis=0, tiled=False)  82.2 us
    dot_general x24, matrix products, mm(): return lax.dot_general(a, b, (dims, ((), ())), preferred_element_type=F32)  62.8 us
    ppermute x36, starting transfers between devices, swap_tp(): return lax.ppermute(x, 'tp', [(i, i ^ j) for i in range(tp_size)])  41.3 us
    unnamed x282, local copies, waits for them, and re-layouts  23.2 us
    dot_general x2, matrix products, attend_backward(): jnp.einsum('bigrd,bjgd->bgrij', grad_heads, value_heads, preferred_elemen...  15.1 us
    all_gather x1, blocking collectives, per_device(): extra = lax.all_gather(extra, zf, axis=0, tiled=False)  13.5 us
    dot_general x2, matrix products, attend_backward(): jnp.einsum('bgrij,bigrd->bjgd', probs.astype(BF16), grad_heads, preferred...  12.1 us
  transfers between devices with their start and end apart: 53, of which 24 were waited for; matrix products, arithmetic and copies ran while one was open for 25% of the time, Pallas kernels for 0%

profile of v1, /device:TPU:0, one launch (start us, length us, event | category | flops | bytes accessed | tf_op | source)
XLA Modules:
  0.0 563.1 jit_solution(22693418035703662)
XLA Ops:
  14.5 13.5 %all_gather.25 = bf16[8,4,128]{2,1,0:T(4,128)(2,1)S(1)} all-gather(bf16[1,4,128]{2,1,0:T(4,128)(2,1)S(1)} %scatter.9), channel_id=1, replica_groups=mesh['seq'=4,'tp'=4,'fsdp'=2] {'seq','fsdp'}, dimensions={0}, use_global_device_ids=true | all-gather | bytes 9216 | tf_op jit(solution)/shard_map/all_gather | solution.py:167
  33.7 8.9 %all-gather.8.cloned.1.call-done = bf16[8,128,512]{2,1,0:T(8,128)(2,1)} async-done(((bf16[2,128,512]{2,1,0:T(8,128)(2,1)}), bf16[8,128,512]{2,1,0:T(8,128)(2,1)}) %all-gather.8.cloned.1.call-update) | async-done | bytes 1048592 | tf_op jit(solution)/shard_map/all_gather | solution.py:176
  52.7 7.8 %collective-permute-done.4 = bf16[4,128,512]{2,1,0:T(8,128)(2,1)S(1)} collective-permute-done((bf16[4,128,512]{2,1,0:T(8,128)(2,1)S(1)}, bf16[4,128,512]{2,1,0:T(8,128)(2,1)S(1)}, u32[]{:S(2)}, u32[]{:S(2)}) %collective-permute-start.4) | collective-permute-done | bytes 524320 | tf_op jit(solution)/shard_map/ppermute | solution.py:117
  62.9 10.3 %collective-permute-done.6 = bf16[4,128,512]{2,1,0:T(8,128)(2,1)S(1)} collective-permute-done((bf16[4,128,512]{2,1,0:T(8,128)(2,1)S(1)}, bf16[4,128,512]{2,1,0:T(8,128)(2,1)S(1)}, u32[]{:S(2)}, u32[]{:S(2)}) %collective-permute-start.6) | collective-permute-done | bytes 524320 | tf_op jit(solution)/shard_map/ppermute | solution.py:117
  75.7 7.4 %collective-permute-done.11 = bf16[4,128,512]{2,1,0:T(8,128)(2,1)S(1)} collective-permute-done((bf16[4,128,512]{2,1,0:T(8,128)(2,1)S(1)}, bf16[4,128,512]{2,1,0:T(8,128)(2,1)S(1)}, u32[]{:S(2)}, u32[]{:S(2)}) %collective-permute-start.11) | collective-permute-done | bytes 524320 | tf_op jit(solution)/shard_map/ppermute | solution.py:117
  83.1 11.5 %collective-permute-done.13 = bf16[4,128,512]{2,1,0:T(8,128)(2,1)S(1)} collective-permute-done((bf16[4,128,512]{2,1,0:T(8,128)(2,1)S(1)}, bf16[4,128,512]{2,1,0:T(8,128)(2,1)S(1)}, u32[]{:S(2)}, u32[]{:S(2)}) %collective-permute-start.13) | collective-permute-done | bytes 524320 | tf_op jit(solution)/shard_map/ppermute | solution.py:117
  104.4 7.6 %fusion.21 = bf16[2048,1024]{0,1:T(8,128)(2,1)S(1)} fusion(bf16[4,2048,1024]{2,1,0:T(8,128)(2,1)} %param.19, s32[]{:T(128)S(6)} %select_n.140, bf16[1024,256]{1,0:T(8,128)(2,1)S(1)} %get-tuple-element.184, bf16[1024,256]{1,0:T(8,128)(2,1)S(1)} %get-tuple-element.182, bf16[1024,256]{1,0:T(8,128)(2,1)S(1)} %get-tuple-element.180, ...), kind=kOutput, calls=%fused_computation.31 | convolution fusion | flops 4305453056 | bytes 10485764 | tf_op jit(solution)/shard_map/dot_general | solution.py:23
  132.2 8.3 %bitcast_reduce_fusion = (f32[8,2,128]{2,1,0:T(2,128)S(1)}, f32[8,2048,128,2]{2,1,3,0:T(8,128)}) fusion(bf16[2048,8,64,1]{0,2,3,1:T(8,128)(2,1)S(1)} %bitcast.416, bf16[128,8,2,64]{0,3,2,1:T(8,128)(2,1)S(1)} %bitcast.425), kind=kOutput, calls=%fused_computation.7 | convolution fusion | flops 545257472 | bytes 19144704 | tf_op jit(solution)/shard_map/bigrd,bjgd->bgrij/dot_general | solution.py:39
  140.5 8.6 %fusion.5 = f32[8,2,128]{2,1,0:T(2,128)S(1)} fusion(f32[8,2048,128,2]{2,1,3,0:T(8,128)} %get-tuple-element.220, f32[8,2,128]{2,1,0:T(2,128)S(1)} %get-tuple-element.219), kind=kLoop, calls=%fused_computation.11 | loop fusion | flops 12580864 | bytes 16793600 | tf_op jit(solution)/shard_map/reduce_sum | solution.py:54
  149.2 8.2 %fusion.63 = bf16[8,64,2,128]{3,1,2,0:T(8,128)(2,1)S(1)} fusion(bf16[2048,8,64,1]{0,2,3,1:T(8,128)(2,1)S(1)} %bitcast.423, f32[8,2,128]{2,1,0:T(2,128)S(1)} %fusion.5, f32[8,2,128]{2,1,0:T(2,128)S(1)} %get-tuple-element.219, f32[8,2048,128,2]{2,1,3,0:T(8,128)} %get-tuple-element.220), kind=kOutput, calls=%fused_computation.104 | convolution fusion | flops 553779200 | bytes 19152896 | tf_op jit(solution)/shard_map/bgrij,bjgd->bigrd/dot_general | solution.py:56
  162.7 5.5 collective-permute-done.17
  168.2 4.4 collective-permute-done.18
  199.2 14.7 %fusion = (f32[8,2,128]{2,1,0:T(2,128)}, f32[8,2048,128,2]{2,1,3,0:T(8,128)}) fusion(f32[8,2048,128,2]{2,1,3,0:T(8,128)} %get-tuple-element.220, f32[8,2,128]{2,1,0:T(2,128)S(1)} %bitcast.490, bf16[2048,8,64,1]{0,2,3,1:T(8,128)(2,1)} %bitcast.422, bf16[128,8,2,64]{0,3,2,1:T(8,128)(2,1)} %bitcast.443), kind=kOutput, calls=%fused_computation.2 | convolution fusion | flops 553646080 | bytes 35930112 | tf_op jit(solution)/shard_map/bigrd,bjgd->bgrij/dot_general | solution.py:64
  216.4 8.1 %fusion.10 = bf16[8,2,128,2048]{2,3,1,0:T(8,128)(2,1)S(1)} fusion(f32[8,2048,128,2]{2,1,3,0:T(8,128)} %get-tuple-element.224, f32[8,2048,128,2]{2,1,3,0:T(8,128)S(1)} %bitcast.415, f32[8,2,128]{2,1,0:T(2,128)} %get-tuple-element.223, f32[8,2,128]{2,1,0:T(2,128)S(1)} %bitcast.491), kind=kLoop, calls=%fused_computation.15 | loop fusion | flops 20971520 | bytes 41959424 | tf_op jit(solution)/shard_map/reshape.150
  229.4 6.1 %fusion.16 = bf16[8,64,2048]{2,1,0:T(8,128)(2,1)S(1)} fusion(bf16[128,8,2,64]{0,3,2,1:T(8,128)(2,1)S(1)} %bitcast.426, bf16[8,2,128,2048]{2,3,1,0:T(8,128)(2,1)} %copy-done), kind=kOutput, calls=%fused_computation.25 | convolution fusion | flops 538968064 | bytes 10747904 | tf_op jit(solution)/shard_map/bgrij,bigrd->bjgd/dot_general | solution.py:74
  235.5 10.2 %bitcast_convert_fusion = bf16[8,64,2048]{2,1,0:T(8,128)(2,1)} fusion(bf16[128,8,2,64]{0,3,2,1:T(8,128)(2,1)S(1)} %bitcast.444, f32[8,2048,128,2]{2,1,3,0:T(8,128)} %get-tuple-element.220, f32[8,2,128]{2,1,0:T(2,128)S(1)} %bitcast.492), kind=kOutput, calls=%fused_computation.23 | convolution fusion | flops 550502400 | bytes 19144704 | tf_op jit(solution)/shard_map/bgrij,bigrd->bjgd/dot_general | solution.py:77
  261.7 8.8 %fusion.42 = bf16[1024,1024]{1,0:T(8,128)(2,1)S(1)} fusion(bf16[2048,1024]{0,1:T(8,128)(2,1)S(1)} %bitcast.429, bf16[4,2048,1024]{2,1,0:T(8,128)(2,1)} %param.19, s32[]{:T(128)S(6)} %select_n.140), kind=kOutput, calls=%fused_computation.66 | convolution fusion | flops 4296015872 | bytes 10485764 | tf_op jit(solution)/shard_map/dot_general | solution.py:23
  315.7 22.3 %collective-permute-done.45 = bf16[4,128,1024]{1,2,0:T(8,128)(2,1)S(1)} collective-permute-done((bf16[4,128,1024]{1,2,0:T(8,128)(2,1)S(1)}, bf16[4,128,1024]{1,2,0:T(8,128)(2,1)S(1)}, u32[]{:S(2)}, u32[]{:S(2)}) %collective-permute-start.45) | collective-permute-done | bytes 1048608 | tf_op jit(solution)/shard_map/ppermute | solution.py:117
  338.0 22.6 %collective-permute-done.46 = bf16[4,128,1024]{1,2,0:T(8,128)(2,1)S(1)} collective-permute-done((bf16[4,128,1024]{1,2,0:T(8,128)(2,1)S(1)}, bf16[4,128,1024]{1,2,0:T(8,128)(2,1)S(1)}, u32[]{:S(2)}, u32[]{:S(2)}) %collective-permute-start.46) | collective-permute-done | bytes 1048608 | tf_op jit(solution)/shard_map/ppermute | solution.py:117
  383.0 4.2 collective-permute-done.20
  419.9 8.5 %collective-permute-done.24 = bf16[128,1024]{1,0:T(8,128)(2,1)} collective-permute-done((bf16[128,1024]{1,0:T(8,128)(2,1)}, bf16[128,1024]{1,0:T(8,128)(2,1)}, u32[]{:S(2)}, u32[]{:S(2)}) %collective-permute-start.24) | collective-permute-done | bytes 262176 | tf_op jit(solution)/shard_map/ppermute | solution.py:117
  433.0 4.3 collective-permute-done.32
  447.9 82.2 %all-gather.2 = f32[32,4,1024]{2,1,0:T(4,128)S(1)} all-gather(f32[1,4,1024]{2,1,0:T(4,128)S(1)} %maximum_bitcast_fusion.2), channel_id=3, replica_groups=mesh['seq'=4,'tp'=4,'fsdp'=2] {'seq','fsdp','tp'}, dimensions={0}, use_global_device_ids=true | all-gather | bytes 540672 | tf_op jit(solution)/shard_map/all_gather | solution.py:331
  531.5 7.4 %collective-permute-done.37 = bf16[128,1024]{1,0:T(8,128)(2,1)S(1)} collective-permute-done((bf16[128,1024]{1,0:T(8,128)(2,1)}, bf16[128,1024]{1,0:T(8,128)(2,1)S(1)}, u32[]{:S(2)}, u32[]{:S(2)}) %collective-permute-start.37) | collective-permute-done | bytes 262176 | tf_op jit(solution)/shard_map/ppermute | solution.py:117
  (559 shorter events, 245.5 us)
Async XLA Ops:
  7.2 35.4 %all-gather.8.cloned.1.call-start = ((), (), s32[]{:S(2)}) async-start(), calls=%async_computation.7 | async-start | bytes 1310720 | tf_op jit(solution)/shard_map/all_gather | solution.py:176
  11.7 102.0 %all-gather.6.cloned.1.call-start = ((), (), s32[]{:S(2)}) async-start(), calls=%async_computation.3 | async-start | bytes 6193152 | tf_op jit(solution)/shard_map/all_gather | solution.py:180
  14.2 533.1 %reduce-scatter.4.cloned.1.call-start = ((), (), s32[]{:S(2)}) async-start(), calls=%async_computation.4 | async-start | bytes 1179648 | tf_op jit(solution)/shard_map/reduce_scatter | solution.py:318
  47.2 26.0 %collective-permute-start.6 = (bf16[4,128,512]{2,1,0:T(8,128)(2,1)S(1)}, bf16[4,128,512]{2,1,0:T(8,128)(2,1)S(1)}, u32[]{:S(2)}, u32[]{:S(2)}) collective-permute-start(bf16[4,128,512]{2,1,0:T(8,128)(2,1)S(1)} %get-tuple-element.177), channel_id=1, source_target_pairs={{0,4},{2,6},{4,0},{6,2},{1,5},{3,7},{5,1},{7,3},{8,12},{10,14},{12... | collective-permute-start | bytes 1572872 | tf_op jit(solution)/shard_map/ppermute | solution.py:117
  48.7 25.4 %collective-permute-start.8 = (bf16[4,128,512]{2,1,0:T(8,128)(2,1)S(1)}, bf16[4,128,512]{2,1,0:T(8,128)(2,1)S(1)}, u32[]{:S(2)}, u32[]{:S(2)}) collective-permute-start(bf16[4,128,512]{2,1,0:T(8,128)(2,1)S(1)} %get-tuple-element.177), channel_id=1, source_target_pairs={{0,6},{2,4},{4,2},{6,0},{1,7},{3,5},{5,3},{7,1},{8,14},{10,12},{12... | collective-permute-start | bytes 1572872 | tf_op jit(solution)/shard_map/ppermute | solution.py:117
  49.3 33.8 %collective-permute-start.11 = (bf16[4,128,512]{2,1,0:T(8,128)(2,1)S(1)}, bf16[4,128,512]{2,1,0:T(8,128)(2,1)S(1)}, u32[]{:S(2)}, u32[]{:S(2)}) collective-permute-start(bf16[4,128,512]{2,1,0:T(8,128)(2,1)S(1)} %get-tuple-element.176), channel_id=1, source_target_pairs={{0,2},{2,0},{4,6},{6,4},{1,3},{3,1},{5,7},{7,5},{8,10},{10,8},{12,... | collective-permute-start | bytes 1572872 | tf_op jit(solution)/shard_map/ppermute | solution.py:117
  50.7 43.8 %collective-permute-start.13 = (bf16[4,128,512]{2,1,0:T(8,128)(2,1)S(1)}, bf16[4,128,512]{2,1,0:T(8,128)(2,1)S(1)}, u32[]{:S(2)}, u32[]{:S(2)}) collective-permute-start(bf16[4,128,512]{2,1,0:T(8,128)(2,1)S(1)} %get-tuple-element.176), channel_id=1, source_target_pairs={{0,4},{2,6},{4,0},{6,2},{1,5},{3,7},{5,1},{7,3},{8,12},{10,14},{12... | collective-permute-start | bytes 1572872 | tf_op jit(solution)/shard_map/ppermute | solution.py:117
  60.6 34.0 %collective-permute-start.15 = (bf16[4,128,512]{2,1,0:T(8,128)(2,1)S(1)}, bf16[4,128,512]{2,1,0:T(8,128)(2,1)S(1)}, u32[]{:S(2)}, u32[]{:S(2)}) collective-permute-start(bf16[4,128,512]{2,1,0:T(8,128)(2,1)S(1)} %get-tuple-element.176), channel_id=1, source_target_pairs={{0,6},{2,4},{4,2},{6,0},{1,7},{3,5},{5,3},{7,1},{8,14},{10,12},{12... | collective-permute-start | bytes 1572872 | tf_op jit(solution)/shard_map/ppermute | solution.py:117
  253.9 51.0 %collective-permute-start.41 = (bf16[4,128,1024]{1,2,0:T(8,128)(2,1)}, bf16[4,128,1024]{1,2,0:T(8,128)(2,1)}, u32[]{:S(2)}, u32[]{:S(2)}) collective-permute-start(bf16[4,128,1024]{1,2,0:T(8,128)(2,1)} %bitcast.460), channel_id=1, source_target_pairs={{0,1},{1,0},{2,3},{3,2},{4,5},{5,4},{6,7},{7,6},{8,9},{9,8},{10,11... | collective-permute-start | bytes 3145736 | tf_op jit(solution)/shard_map/ppermute | solution.py:120
  259.2 47.6 %collective-permute-start.42 = (bf16[4,128,1024]{1,2,0:T(8,128)(2,1)}, bf16[4,128,1024]{1,2,0:T(8,128)(2,1)}, u32[]{:S(2)}, u32[]{:S(2)}) collective-permute-start(bf16[4,128,1024]{1,2,0:T(8,128)(2,1)} %bitcast.459), channel_id=1, source_target_pairs={{0,1},{1,0},{2,3},{3,2},{4,5},{5,4},{6,7},{7,6},{8,9},{9,8},{10,11... | collective-permute-start | bytes 3145736 | tf_op jit(solution)/shard_map/ppermute | solution.py:120
  304.8 244.8 %reduce-scatter.6.cloned.1.call-start = ((), (), s32[]{:S(2)}) async-start(), calls=%async_computation.5 | async-start | bytes 1310720 | tf_op jit(solution)/shard_map/reduce_scatter | solution.py:309
  311.9 26.1 %collective-permute-start.45 = (bf16[4,128,1024]{1,2,0:T(8,128)(2,1)S(1)}, bf16[4,128,1024]{1,2,0:T(8,128)(2,1)S(1)}, u32[]{:S(2)}, u32[]{:S(2)}) collective-permute-start(bf16[4,128,1024]{1,2,0:T(8,128)(2,1)S(1)} %pad_maximum_fusion.17), channel_id=1, source_target_pairs={{0,2},{2,0},{4,6},{6,4},{1,3},{3,1},{5,7},{7,5},{8,10},{10,8},{12,... | collective-permute-start | bytes 3145736 | tf_op jit(solution)/shard_map/ppermute | solution.py:117
  313.3 47.3 %collective-permute-start.46 = (bf16[4,128,1024]{1,2,0:T(8,128)(2,1)S(1)}, bf16[4,128,1024]{1,2,0:T(8,128)(2,1)S(1)}, u32[]{:S(2)}, u32[]{:S(2)}) collective-permute-start(bf16[4,128,1024]{1,2,0:T(8,128)(2,1)S(1)} %pad_maximum_fusion.18), channel_id=1, source_target_pairs={{0,4},{2,6},{4,0},{6,2},{1,5},{3,7},{5,1},{7,3},{8,12},{10,14},{12... | collective-permute-start | bytes 3145736 | tf_op jit(solution)/shard_map/ppermute | solution.py:117
  314.2 46.4 %collective-permute-start.47 = (bf16[4,128,1024]{1,2,0:T(8,128)(2,1)S(1)}, bf16[4,128,1024]{1,2,0:T(8,128)(2,1)S(1)}, u32[]{:S(2)}, u32[]{:S(2)}) collective-permute-start(bf16[4,128,1024]{1,2,0:T(8,128)(2,1)S(1)} %pad_maximum_fusion.19), channel_id=1, source_target_pairs={{0,6},{2,4},{4,2},{6,0},{1,7},{3,5},{5,3},{7,1},{8,14},{10,12},{12... | collective-permute-start | bytes 3145736 | tf_op jit(solution)/shard_map/ppermute | solution.py:117
  362.2 190.6 %reduce-scatter.8.cloned.1.call-start = ((), (), s32[]{:S(2)}) async-start(), calls=%async_computation.6 | async-start | bytes 5013504 | tf_op jit(solution)/shard_map/reduce_scatter | solution.py:256
  394.3 23.0 %collective-permute-start.23 = (bf16[128,1024]{1,0:T(8,128)(2,1)}, bf16[128,1024]{1,0:T(8,128)(2,1)}, u32[]{:S(2)}, u32[]{:S(2)}) collective-permute-start(bf16[128,1024]{1,0:T(8,128)(2,1)} %get-tuple-element.113), channel_id=1, source_target_pairs={{0,2},{2,0},{4,6},{6,4},{1,3},{3,1},{5,7},{7,5},{8,10},{10,8},{12,... | collective-permute-start | bytes 786440 | tf_op jit(solution)/shard_map/ppermute | solution.py:117
  395.3 33.1 %collective-permute-start.24 = (bf16[128,1024]{1,0:T(8,128)(2,1)}, bf16[128,1024]{1,0:T(8,128)(2,1)}, u32[]{:S(2)}, u32[]{:S(2)}) collective-permute-start(bf16[128,1024]{1,0:T(8,128)(2,1)} %get-tuple-element.113), channel_id=1, source_target_pairs={{0,4},{2,6},{4,0},{6,2},{1,5},{3,7},{5,1},{7,3},{8,12},{10,14},{12... | collective-permute-start | bytes 786440 | tf_op jit(solution)/shard_map/ppermute | solution.py:117
  396.2 34.4 %collective-permute-start.25 = (bf16[128,1024]{1,0:T(8,128)(2,1)}, bf16[128,1024]{1,0:T(8,128)(2,1)}, u32[]{:S(2)}, u32[]{:S(2)}) collective-permute-start(bf16[128,1024]{1,0:T(8,128)(2,1)} %get-tuple-element.113), channel_id=1, source_target_pairs={{0,6},{2,4},{4,2},{6,0},{1,7},{3,5},{5,3},{7,1},{8,14},{10,12},{12... | collective-permute-start | bytes 786440 | tf_op jit(solution)/shard_map/ppermute | solution.py:117
  400.1 144.9 %collective-permute-start.40 = (bf16[2048,256]{1,0:T(8,128)(2,1)}, bf16[2048,256]{1,0:T(8,128)(2,1)}, u32[]{:S(2)}, u32[]{:S(2)}) collective-permute-start(bf16[2048,256]{1,0:T(8,128)(2,1)} %convolution_convert_fusion.1), channel_id=1, source_target_pairs={{0,6},{2,4},{4,2},{6,0},{1,7},{3,5},{5,3},{7,1},{8,14},{10,12},{12... | collective-permute-start | bytes 3145736 | tf_op jit(solution)/shard_map/ppermute | solution.py:117
  413.7 23.7 %collective-permute-start.32 = (bf16[128,1024]{1,0:T(8,128)(2,1)}, bf16[128,1024]{1,0:T(8,128)(2,1)S(1)}, u32[]{:S(2)}, u32[]{:S(2)}) collective-permute-start(bf16[128,1024]{1,0:T(8,128)(2,1)} %get-tuple-element.147), channel_id=1, source_target_pairs={{0,2},{2,0},{4,6},{6,4},{1,3},{3,1},{5,7},{7,5},{8,10},{10,8},{12,... | collective-permute-start | bytes 786440 | tf_op jit(solution)/shard_map/ppermute | solution.py:117
  430.6 112.2 %collective-permute-start.39 = (bf16[2048,256]{1,0:T(8,128)(2,1)}, bf16[2048,256]{1,0:T(8,128)(2,1)}, u32[]{:S(2)}, u32[]{:S(2)}) collective-permute-start(bf16[2048,256]{1,0:T(8,128)(2,1)} %convolution_convert_fusion.2), channel_id=1, source_target_pairs={{0,4},{2,6},{4,0},{6,2},{1,5},{3,7},{5,1},{7,3},{8,12},{10,14},{12... | collective-permute-start | bytes 3145736 | tf_op jit(solution)/shard_map/ppermute | solution.py:117
  437.4 103.2 %collective-permute-start.38 = (bf16[2048,256]{1,0:T(8,128)(2,1)}, bf16[2048,256]{1,0:T(8,128)(2,1)}, u32[]{:S(2)}, u32[]{:S(2)}) collective-permute-start(bf16[2048,256]{1,0:T(8,128)(2,1)} %convolution_convert_fusion.3), channel_id=1, source_target_pairs={{0,2},{2,0},{4,6},{6,4},{1,3},{3,1},{5,7},{7,5},{8,10},{10,8},{12,... | collective-permute-start | bytes 3145736 | tf_op jit(solution)/shard_map/ppermute | solution.py:117
  446.0 85.5 %collective-permute-start.35 = (bf16[128,1024]{1,0:T(8,128)(2,1)}, bf16[128,1024]{1,0:T(8,128)(2,1)S(1)}, u32[]{:S(2)}, u32[]{:S(2)}) collective-permute-start(bf16[128,1024]{1,0:T(8,128)(2,1)} %get-tuple-element.111), channel_id=1, source_target_pairs={{0,2},{2,0},{4,6},{6,4},{1,3},{3,1},{5,7},{7,5},{8,10},{10,8},{12,... | collective-permute-start | bytes 786440 | tf_op jit(solution)/shard_map/ppermute | solution.py:117
  446.7 84.8 %collective-permute-start.36 = (bf16[128,1024]{1,0:T(8,128)(2,1)}, bf16[128,1024]{1,0:T(8,128)(2,1)S(1)}, u32[]{:S(2)}, u32[]{:S(2)}) collective-permute-start(bf16[128,1024]{1,0:T(8,128)(2,1)} %get-tuple-element.111), channel_id=1, source_target_pairs={{0,4},{2,6},{4,0},{6,2},{1,5},{3,7},{5,1},{7,3},{8,12},{10,14},{12... | collective-permute-start | bytes 786440 | tf_op jit(solution)/shard_map/ppermute | solution.py:117
  (164 other events, 1573.6 us)
Sparse Core Ops, SparseCore 0:
  11.8 30.7 all-gather.7
  44.8 57.5 all-gather.5
  304.9 31.2 reduce-scatter.3
  362.3 25.7 reduce-scatter.5
  390.2 50.8 reduce-scatter.7
